TPU v7x, 32 devices: a whole 2x2x4 slice. The times are simulated.
32 devices in a mesh: pts: 8 (over y, x, core), val: 4 (over z).
Axes of the slice: x: 2, y: 2, z: 4, core: 2. Of those that a mesh axis runs over, the one named last changes fastest.
Arguments:
- vectors: float32 [1, 512, 2048], P(None, 'val', 'pts'), may hold values from -6 to 6
- eval_energy: float32 [512], P('val'), may hold values from -2 to -0.2
- cond_energy: float32 [2048], P('pts'), may hold values from 0.2 to 2
- val_orbitals: float32 [512, 8192], P('pts', 'val'), may hold values from -0.25 to 0.25
- cond_orbitals: float32 [2048, 8192], P('val', 'pts'), may hold values from -0.125 to 0.125
- screened: float32 [8192, 8192], P('val', 'pts'), may hold values from -1.5 to 1.5
Outputs:
- filtered: float32 [1, 512, 2048], P(None, 'val', 'pts')
All inputs are finite; a program needn't handle non-finite values.
Results may differ from a plain program's by a relative error of at most 0.00013.
Values sent between devices are 32-bit elements; how exact they have to be, the bound alone decides.
A program may use at most 128 MiB of HBM per device.

v0:
```python
import jax
import jax.numpy as jnp
from jax import lax
from jax.sharding import PartitionSpec as P

ITERS = 2
CENTER = 2.2
HALF_WIDTH = 2.0


def per_device(vectors, eval_energy, cond_energy, val_orbitals, cond_orbitals, screened):
    highest = lax.Precision.HIGHEST
    cond_whole = lax.all_gather(cond_orbitals, "val", axis=0, tiled=True)
    val_whole = lax.all_gather(val_orbitals, "pts", axis=0, tiled=True)
    ediff = cond_energy[None, None, :] - eval_energy[None, :, None]
    older = vectors
    newer = vectors
    for step in range(ITERS):
        direct_full_x = lax.all_gather(newer, "pts", axis=2, tiled=True)
        pair = jnp.einsum(
            "bvc,cn->bvn",
            direct_full_x,
            cond_whole,
            precision=highest,
            preferred_element_type=jnp.float32,
        )
        pair_all = lax.all_gather(pair, "val", axis=1, tiled=True)
        mixed = jnp.einsum(
            "vm,bvn->bmn",
            val_whole,
            pair_all,
            precision=highest,
            preferred_element_type=jnp.float32,
        )
        weighted = mixed * screened[None, :, :]
        back_terms = jnp.einsum(
            "vm,bmn->bvn",
            val_whole,
            weighted,
            precision=highest,
            preferred_element_type=jnp.float32,
        )
        back = lax.psum_scatter(back_terms, "val", scatter_dimension=1, tiled=True)
        hamil = ediff * newer - lax.psum_scatter(
            jnp.einsum(
                "bvn,cn->bvc",
                back,
                cond_whole,
                precision=highest,
                preferred_element_type=jnp.float32,
            ),
            "pts",
            scatter_dimension=2,
            tiled=True,
        )
        scaled = (hamil - CENTER * newer) / HALF_WIDTH
        if step == 0:
            following = scaled
        else:
            following = 2.0 * scaled - older
        older = newer
        newer = following
    return newer


def solution(mesh):
    placed = (
        P(None, "val", "pts"),
        P("val"),
        P("pts"),
        P("pts", "val"),
        P("val", "pts"),
        P("val", "pts"),
    )
    return jax.shard_map(
        per_device, mesh=mesh, in_specs=placed, out_specs=P(None, "val", "pts"), check_vma=False
    )
```

profile of v0, /device:TPU:0, one launch (start us, length us, event | category | flops | bytes accessed | tf_op | source)
XLA Modules:
  0.0 608.8 jit_solution(13954029730441035257)
XLA Ops:
  6.5 0.7 all-gather.9.cloned.1.call-update
  7.3 0.0 all-gather.11.cloned.1.call-start
  7.3 0.7 all-gather.11.cloned.1.call-update
  8.1 0.7 all-gather.13.cloned.1.call-update
  8.7 0.0 all-gather.17.cloned.1.call-start
  8.8 26.7 %all-gather.9.cloned.1.call-done = f32[1,128,2048]{2,1,0:T(8,128)} async-done(((f32[1,128,256]{2,1,0:T(8,128)}), f32[1,128,2048]{2,1,0:T(8,128)}) %all-gather.9.cloned.1.call-update) | async-done | bytes 1048592 | tf_op jit(solution)/shard_map/all_gather | solution.py:19
  35.4 151.2 %all-gather.11.cloned.1.call-done = f32[2048,1024]{1,0:T(8,128)} async-done(((f32[512,1024]{1,0:T(8,128)}), f32[2048,1024]{1,0:T(8,128)}) %all-gather.11.cloned.1.call-update) | async-done | bytes 8388624 | tf_op jit(solution)/shard_map/all_gather | solution.py:13
  186.7 9.2 %fusion.16 = f32[128,1024]{1,0:T(8,128)} fusion(f32[2048,1024]{1,0:T(8,128)} %all-gather.11.cloned.1.call-done, f32[1,128,2048]{2,1,0:T(8,128)} %all-gather.9.cloned.1.call-done), kind=kOutput, calls=%fused_computation.14 | convolution fusion | flops 3221225472 | bytes 9961472 | tf_op jit(solution)/shard_map/bvc,cn->bvn/dot_general | solution.py:20
  195.8 0.2 reduce-scatter.5.cloned.1.call-start
  196.1 9.1 %copy.7 = f32[2048,1024]{0,1:T(8,128)} copy(f32[2048,1024]{1,0:T(8,128)} %param.11) | data formatting | bytes 16777216 | tf_op args[5]
  205.2 18.1 %all-gather.13.cloned.1.call-done = f32[512,2048]{1,0:T(8,128)} async-done(((f32[64,2048]{1,0:T(8,128)}), f32[512,2048]{1,0:T(8,128)}) %all-gather.13.cloned.1.call-update) | async-done | bytes 4194320 | tf_op jit(solution)/shard_map/all_gather | solution.py:14
  223.3 47.1 %all-gather.17.cloned.1.call-done = f32[512,1024]{1,0:T(8,128)} async-done(((f32[128,1024]{1,0:T(8,128)}), f32[512,1024]{1,0:T(8,128)}) %all-gather.17.cloned.1.call-update) | async-done | bytes 2097168 | tf_op jit(solution)/shard_map/all_gather | solution.py:27
  270.5 17.0 %fusion.26 = f32[1024,2048]{1,0:T(8,128)S(1)} fusion(f32[512,1024]{1,0:T(8,128)} %all-gather.17.cloned.1.call-done, f32[512,2048]{1,0:T(8,128)} %all-gather.13.cloned.1.call-done), kind=kOutput, calls=%fused_computation.26 | convolution fusion | flops 12884901888 | bytes 14680064 | tf_op jit(solution)/shard_map/vm,bvn->bmn/dot_general | solution.py:28
  287.5 15.3 %fusion.8 = f32[1,512,1024]{1,2,0:T(8,128)} fusion(f32[512,2048]{1,0:T(8,128)S(1)} %copy-done.1, f32[1024,2048]{1,0:T(8,128)S(1)} %fusion.26, f32[2048,1024]{0,1:T(8,128)S(1)} %copy-done), kind=kOutput, calls=%fused_computation.10 | convolution fusion | flops 12886999040 | bytes 23068672 | tf_op jit(solution)/shard_map/vm,bmn->bvn/dot_general | solution.py:36
  302.8 0.3 reduce-scatter.7.cloned.1.call-start
  303.1 42.3 %reduce-scatter.5.cloned.1.call-done = f32[1,128,1024]{1,2,0:T(8,128)} async-done(((f32[1,512,1024]{1,2,0:T(8,128)}), f32[1,128,1024]{1,2,0:T(8,128)}) %reduce-scatter.5.cloned.1.call-update) | async-done | bytes 524304 | tf_op jit(solution)/shard_map/reduce_scatter | solution.py:43
  345.4 13.4 %convolution_bitcast_fusion.1 = f32[1,128,2048]{2,1,0:T(8,128)} fusion(f32[2048,1024]{1,0:T(8,128)} %all-gather.11.cloned.1.call-done, f32[1,128,1024]{1,2,0:T(8,128)} %reduce-scatter.5.cloned.1.call-done), kind=kOutput, calls=%fused_computation.9 | convolution fusion | flops 3221225472 | bytes 9961472 | tf_op jit(solution)/shard_map/bvn,cn->bvc/dot_general | solution.py:45
  358.8 0.0 all-gather.15.cloned.1.call-start
  358.8 35.3 %reduce-scatter.7.cloned.1.call-done = f32[1,128,256]{2,1,0:T(8,128)} async-done(((f32[1,128,2048]{2,1,0:T(8,128)}), f32[1,128,256]{2,1,0:T(8,128)}) %reduce-scatter.7.cloned.1.call-update) | async-done | bytes 131088 | tf_op jit(solution)/shard_map/reduce_scatter | solution.py:44
  394.1 1.7 fusion.25
  395.8 0.0 all-gather.19.cloned.1.call-start
  395.8 23.6 %all-gather.15.cloned.1.call-done = f32[1,128,2048]{2,1,0:T(8,128)} async-done(((f32[1,128,256]{2,1,0:T(8,128)}), f32[1,128,2048]{2,1,0:T(8,128)}) %all-gather.15.cloned.1.call-update) | async-done | bytes 1048592 | tf_op jit(solution)/shard_map/all_gather | solution.py:19
  419.5 9.2 %fusion.14 = f32[128,1024]{1,0:T(8,128)} fusion(f32[2048,1024]{1,0:T(8,128)} %all-gather.11.cloned.1.call-done, f32[1,128,2048]{2,1,0:T(8,128)} %all-gather.15.cloned.1.call-done), kind=kOutput, calls=%fused_computation.12 | convolution fusion | flops 3221225472 | bytes 9961472 | tf_op jit(solution)/shard_map/bvc,cn->bvn/dot_general | solution.py:20
  428.7 0.4 reduce-scatter.9.cloned.1.call-start
  429.1 45.4 %all-gather.19.cloned.1.call-done = f32[512,1024]{1,0:T(8,128)} async-done(((f32[128,1024]{1,0:T(8,128)}), f32[512,1024]{1,0:T(8,128)}) %all-gather.19.cloned.1.call-update) | async-done | bytes 2097168 | tf_op jit(solution)/shard_map/all_gather | solution.py:27
  474.5 16.9 %fusion.27 = f32[1024,2048]{1,0:T(8,128)S(1)} fusion(f32[512,1024]{1,0:T(8,128)} %all-gather.19.cloned.1.call-done, f32[512,2048]{1,0:T(8,128)} %all-gather.13.cloned.1.call-done), kind=kOutput, calls=%fused_computation.27 | convolution fusion | flops 12884901888 | bytes 14680064 | tf_op jit(solution)/shard_map/vm,bvn->bmn/dot_general | solution.py:28
  491.4 17.3 %fusion.11 = f32[1,512,1024]{1,2,0:T(8,128)} fusion(f32[512,2048]{1,0:T(8,128)S(1)} %copy-done.2, f32[1024,2048]{1,0:T(8,128)S(1)} %fusion.27, f32[2048,1024]{0,1:T(8,128)} %copy.7), kind=kOutput, calls=%fused_computation.11 | convolution fusion | flops 12886999040 | bytes 23068672 | tf_op jit(solution)/shard_map/vm,bmn->bvn/dot_general | solution.py:36
  508.7 0.2 reduce-scatter.11.cloned.1.call-start
  508.9 42.4 %reduce-scatter.9.cloned.1.call-done = f32[1,128,1024]{1,2,0:T(8,128)} async-done(((f32[1,512,1024]{1,2,0:T(8,128)}), f32[1,128,1024]{1,2,0:T(8,128)}) %reduce-scatter.9.cloned.1.call-update) | async-done | bytes 524304 | tf_op jit(solution)/shard_map/reduce_scatter | solution.py:43
  551.3 13.4 %convolution_bitcast_fusion = f32[1,128,2048]{2,1,0:T(8,128)} fusion(f32[2048,1024]{1,0:T(8,128)} %all-gather.11.cloned.1.call-done, f32[1,128,1024]{1,2,0:T(8,128)} %reduce-scatter.9.cloned.1.call-done), kind=kOutput, calls=%fused_computation.8 | convolution fusion | flops 3221225472 | bytes 9961472 | tf_op jit(solution)/shard_map/bvn,cn->bvc/dot_general | solution.py:45
  564.8 35.3 %reduce-scatter.11.cloned.1.call-done = f32[1,128,256]{2,1,0:T(8,128)} async-done(((f32[1,128,2048]{2,1,0:T(8,128)}), f32[1,128,256]{2,1,0:T(8,128)}) %reduce-scatter.11.cloned.1.call-update) | async-done | bytes 131088 | tf_op jit(solution)/shard_map/reduce_scatter | solution.py:44
  600.1 1.7 fusion.24
  (23 shorter events, 0.2 us)
Async XLA Ops:
  6.5 28.9 %all-gather.9.cloned.1.call-start = ((), (), s32[]{:S(2)}) async-start(), calls=%async_computation.4 | async-start | bytes 1179648 | tf_op jit(solution)/shard_map/all_gather | solution.py:19
  7.3 179.4 %all-gather.11.cloned.1.call-start = ((), (), s32[]{:S(2)}) async-start(), calls=%async_computation.5 | async-start | bytes 10485760 | tf_op jit(solution)/shard_map/all_gather | solution.py:13
  8.0 215.3 %all-gather.13.cloned.1.call-start = ((), (), s32[]{:S(2)}) async-start(), calls=%async_computation.6 | async-start | bytes 4718592 | tf_op jit(solution)/shard_map/all_gather | solution.py:14
  8.7 261.7 %all-gather.17.cloned.1.call-start = ((), (), s32[]{:S(2)}) async-start(), calls=%async_computation.12 | async-start | bytes 2621440 | tf_op jit(solution)/shard_map/all_gather | solution.py:27
  195.8 149.5 %reduce-scatter.5.cloned.1.call-start = ((), (), s32[]{:S(2)}) async-start(), calls=%async_computation.7 | async-start | bytes 2621440 | tf_op jit(solution)/shard_map/reduce_scatter | solution.py:43
  270.5 17.0 %copy-start = (f32[2048,1024]{0,1:T(8,128)S(1)}, f32[2048,1024]{0,1:T(8,128)}, u32[]{:S(2)}) copy-start(f32[2048,1024]{0,1:T(8,128)} %copy.7) | copy-start | bytes 25165828
  270.5 17.0 %copy-start.1 = (f32[512,2048]{1,0:T(8,128)S(1)}, f32[512,2048]{1,0:T(8,128)}, u32[]{:S(2)}) copy-start(f32[512,2048]{1,0:T(8,128)} %all-gather.13.cloned.1.call-done) | copy-start | bytes 12582916
  302.8 91.3 %copy-start.3 = (f32[1,128,256]{2,1,0:T(8,128)S(1)}, f32[1,128,256]{2,1,0:T(8,128)}, u32[]{:S(2)}) copy-start(f32[1,128,256]{2,1,0:T(8,128)} %param.6) | copy-start | bytes 393220
  302.8 91.3 %copy-start.5 = (f32[256]{0:T(256)S(1)}, f32[256]{0:T(256)}, u32[]{:S(2)}) copy-start(f32[256]{0:T(256)} %param.8) | copy-start | bytes 3076
  302.8 91.3 %copy-start.6 = (f32[128]{0:T(128)S(1)}, f32[128]{0:T(128)}, u32[]{:S(2)}) copy-start(f32[128]{0:T(128)} %param.7) | copy-start | bytes 1540
  302.8 91.3 %reduce-scatter.7.cloned.1.call-start = ((), (), s32[]{:S(2)}) async-start(), calls=%async_computation.8 | async-start | bytes 1179648 | tf_op jit(solution)/shard_map/reduce_scatter | solution.py:44
  358.8 60.7 %all-gather.15.cloned.1.call-start = ((), (), s32[]{:S(2)}) async-start(), calls=%async_computation.9 | async-start | bytes 1179648 | tf_op jit(solution)/shard_map/all_gather | solution.py:19
  395.8 78.7 %all-gather.19.cloned.1.call-start = ((), (), s32[]{:S(2)}) async-start(), calls=%async_computation.13 | async-start | bytes 2621440 | tf_op jit(solution)/shard_map/all_gather | solution.py:27
  428.7 122.7 %reduce-scatter.9.cloned.1.call-start = ((), (), s32[]{:S(2)}) async-start(), calls=%async_computation.10 | async-start | bytes 2621440 | tf_op jit(solution)/shard_map/reduce_scatter | solution.py:43
  474.5 17.0 %copy-start.2 = (f32[512,2048]{1,0:T(8,128)S(1)}, f32[512,2048]{1,0:T(8,128)}, u32[]{:S(2)}) copy-start(f32[512,2048]{1,0:T(8,128)} %all-gather.13.cloned.1.call-done) | copy-start | bytes 12582916
  508.7 91.4 %copy-start.4 = (f32[1,128,256]{2,1,0:T(8,128)S(1)}, f32[1,128,256]{2,1,0:T(8,128)}, u32[]{:S(2)}) copy-start(f32[1,128,256]{2,1,0:T(8,128)} %reduce-scatter.7.cloned.1.call-done) | copy-start | bytes 393220
  508.7 91.4 %reduce-scatter.11.cloned.1.call-start = ((), (), s32[]{:S(2)}) async-start(), calls=%async_computation.11 | async-start | bytes 1179648 | tf_op jit(solution)/shard_map/reduce_scatter | solution.py:44
Sparse Core Ops, SparseCore 0:
  9.2 26.1 all-gather.8
  37.0 149.5 all-gather.10
  188.5 34.7 all-gather.12
  224.8 45.6 all-gather.16
  302.9 42.4 reduce-scatter.4
  358.9 35.1 reduce-scatter.6
  396.0 23.4 all-gather.14
  428.8 45.6 all-gather.18
  508.8 42.4 reduce-scatter.8
  564.9 35.1 reduce-scatter.10
where the time goes:
time: 613 us; the launch traced here: 609 us
  waiting for transfers between devices  470 us (77%)
  matrix products  112 us (18%)
  between operations  13.8 us (2%)
  local copies, waits for them, and re-layouts  9.17 us (1%)
    all_gather x1, waiting for transfers between devices, per_device(): cond_whole = lax.all_gather(cond_orbitals, 'val', axis=0, tiled=True)  151 us
    all_gather x2, waiting for transfers between devices, per_device(): pair_all = lax.all_gather(pair, 'val', axis=1, tiled=True)  92.5 us
    reduce_scatter x2, waiting for transfers between devices, per_device(): back = lax.psum_scatter(back_terms, 'val', scatter_dimension=1, tiled=True)  84.7 us
    reduce_scatter x2, waiting for transfers between devices, per_device(): lax.psum_scatter(jnp.einsum('bvn,cn->bvc', back, cond_whole, precision=hi...  70.5 us
    all_gather x2, waiting for transfers between devices, per_device(): direct_full_x = lax.all_gather(newer, 'pts', axis=2, tiled=True)  50.3 us
    dot_general x2, matrix products, per_device(): jnp.einsum('vm,bvn->bmn', val_whole, pair_all, precision=highest, preferr...  33.9 us
    dot_general x2, matrix products, per_device(): jnp.einsum('vm,bmn->bvn', val_whole, weighted, precision=highest, preferr...  32.6 us
    dot_general x2, matrix products, per_device(): jnp.einsum('bvn,cn->bvc', back, cond_whole, precision=highest, preferred_...  26.8 us
  transfers between devices with their start and end apart: 10, of which 10 were waited for; matrix products, arithmetic and copies ran while one was open for 3% of the time, Pallas kernels for 0%

commit v1 on v0

--- a/solution.py
+++ b/solution.py
@@ -24,7 +24,18 @@
             precision=highest,
             preferred_element_type=jnp.float32,
         )
-        pair_all = lax.all_gather(pair, "val", axis=1, tiled=True)
+        num = lax.axis_size("val")
+        blocks_here = [pair]
+        for b in range(num - 1):
+            m_next = lax.ppermute(
+                blocks_here[-1], axis_name="val", perm=[(u, (u + 1) % num) for u in range(num)]
+            )
+            blocks_here.append(m_next)
+        pair_all = jnp.roll(
+            jnp.concatenate(blocks_here[::-1], axis=1),
+            shift=(lax.axis_index("val") + 1) * pair.shape[1],
+            axis=1,
+        )
         mixed = jnp.einsum(
             "vm,bvn->bmn",
             val_whole,

time: 613 us -> 577 us (0.941)
  waiting for transfers between devices: 470 us -> 435 us
    all_gather x2 -> x0, waiting for transfers between devices: 92.5 us -> none  [per_device(): pair_all = lax.all_gather(pair, 'val', axis=1, tiled=True)]
    ppermute x0 -> x6, waiting for transfers between devices: none -> 78.7 us  [per_device(): lax.ppermute(blocks_here[-1], axis_name='val', perm=[(u, (u + 1) % num) f...]
    all_gather x1, waiting for transfers between devices: 18.1 us -> 0.01 us  [per_device(): val_whole = lax.all_gather(val_orbitals, 'pts', axis=0, tiled=True)]
  transfers between devices with their start and end apart: 10 -> 14, of which waited for: 10 -> 13; matrix products, arithmetic and copies ran while one was open for 3% -> 3% of each run, Pallas kernels for 0% -> 0%
where the time goes in v1:
time: 577 us; the launch traced here: 574 us
  waiting for transfers between devices  435 us (75%)
  matrix products  110 us (19%)
  between operations  13.9 us (2%)
  local copies, waits for them, and re-layouts  9.19 us (2%)
    all_gather x1, waiting for transfers between devices, per_device(): cond_whole = lax.all_gather(cond_orbitals, 'val', axis=0, tiled=True)  151 us
    reduce_scatter x2, waiting for transfers between devices, per_device(): back = lax.psum_scatter(back_terms, 'val', scatter_dimension=1, tiled=True)  82.5 us
    ppermute x6, waiting for transfers between devices, per_device(): lax.ppermute(blocks_here[-1], axis_name='val', perm=[(u, (u + 1) % num) f...  78.7 us
    reduce_scatter x2, waiting for transfers between devices, per_device(): lax.psum_scatter(jnp.einsum('bvn,cn->bvc', back, cond_whole, precision=hi...  70.6 us
    all_gather x2, waiting for transfers between devices, per_device(): direct_full_x = lax.all_gather(newer, 'pts', axis=2, tiled=True)  50.2 us
    dot_general x2, matrix products, per_device(): jnp.einsum('vm,bvn->bmn', val_whole, pair_all, precision=highest, preferr...  36.9 us
    dot_general x2, matrix products, per_device(): jnp.einsum('vm,bmn->bvn', val_whole, weighted, precision=highest, preferr...  30.9 us
    dot_general x2, matrix products, per_device(): jnp.einsum('bvn,cn->bvc', back, cond_whole, precision=highest, preferred_...  26.8 us
  transfers between devices with their start and end apart: 14, of which 13 were waited for; matrix products, arithmetic and copies ran while one was open for 3% of the time, Pallas kernels for 0%

profile of v1, /device:TPU:0, one launch (start us, length us, event | category | flops | bytes accessed | tf_op | source)
XLA Modules:
  0.0 574.3 jit_solution(6192828571499579017)
XLA Ops:
  6.5 0.7 all-gather.5.cloned.1.call-update
  7.3 0.7 all-gather.7.cloned.1.call-update
  8.1 0.7 all-gather.9.cloned.1.call-update
  8.8 26.7 %all-gather.5.cloned.1.call-done = f32[1,128,2048]{2,1,0:T(8,128)} async-done(((f32[1,128,256]{2,1,0:T(8,128)}), f32[1,128,2048]{2,1,0:T(8,128)}) %all-gather.5.cloned.1.call-update) | async-done | bytes 1048592 | tf_op jit(solution)/shard_map/all_gather | solution.py:19
  35.4 151.2 %all-gather.7.cloned.1.call-done = f32[2048,1024]{1,0:T(8,128)} async-done(((f32[512,1024]{1,0:T(8,128)}), f32[2048,1024]{1,0:T(8,128)}) %all-gather.7.cloned.1.call-update) | async-done | bytes 8388624 | tf_op jit(solution)/shard_map/all_gather | solution.py:13
  186.7 7.5 %convolution_bitcast_fusion.3 = f32[1,128,1024]{2,1,0:T(8,128)S(1)} fusion(f32[2048,1024]{1,0:T(8,128)} %all-gather.7.cloned.1.call-done, f32[1,128,2048]{2,1,0:T(8,128)} %all-gather.5.cloned.1.call-done), kind=kOutput, calls=%fused_computation.47 | convolution fusion | flops 3221225472 | bytes 9961472 | tf_op jit(solution)/shard_map/bvc,cn->bvn/dot_general | solution.py:20
  194.2 0.1 collective-permute-start
  194.2 15.6 %collective-permute-done = f32[1,128,1024]{2,1,0:T(8,128)S(1)} collective-permute-done((f32[1,128,1024]{2,1,0:T(8,128)S(1)}, f32[1,128,1024]{2,1,0:T(8,128)S(1)}, u32[]{:S(2)}, u32[]{:S(2)}) %collective-permute-start) | collective-permute-done | bytes 524320 | tf_op jit(solution)/shard_map/ppermute | solution.py:30
  209.8 14.8 %collective-permute-done.1 = f32[1,128,1024]{2,1,0:T(8,128)S(1)} collective-permute-done((f32[1,128,1024]{2,1,0:T(8,128)S(1)}, f32[1,128,1024]{2,1,0:T(8,128)S(1)}, u32[]{:S(2)}, u32[]{:S(2)}) %collective-permute-start.1) | collective-permute-done | bytes 524320 | tf_op jit(solution)/shard_map/ppermute | solution.py:30
  224.6 0.2 collective-permute-start.2
  224.8 9.1 %copy.7 = f32[2048,1024]{0,1:T(8,128)} copy(f32[2048,1024]{1,0:T(8,128)} %param.13) | data formatting | bytes 16777216 | tf_op args[5]
  233.9 4.7 collective-permute-done.2
  238.7 20.1 %fusion.24 = f32[1024,2048]{1,0:T(8,128)S(1)} fusion(f32[512,2048]{1,0:T(8,128)} %all-gather.9.cloned.1.call-done, s32[]{:T(128)S(6)} %select_n.13, f32[1,128,1024]{2,1,0:T(8,128)S(1)} %collective-permute-done.2, f32[1,128,1024]{2,1,0:T(8,128)S(1)} %collective-permute-done.1, f32[1,128,1024]{2,1,0:T(8,128)S(1)} %collective-permute-done, ...), kind=kOutput, calls=%fused_computation.40 | convolution fusion | flops 12888571904 | bytes 14680068 | tf_op jit(solution)/shard_map/vm,bvn->bmn/dot_general | solution.py:39
  258.8 15.5 %fusion.30 = f32[1,512,1024]{1,2,0:T(8,128)} fusion(f32[512,2048]{1,0:T(8,128)S(1)} %copy-done.1, f32[1024,2048]{1,0:T(8,128)S(1)} %fusion.24, f32[2048,1024]{0,1:T(8,128)S(1)} %copy-done), kind=kOutput, calls=%fused_computation.44 | convolution fusion | flops 12886999040 | bytes 23068672 | tf_op jit(solution)/shard_map/vm,bmn->bvn/dot_general | solution.py:47
  274.5 41.8 %reduce-scatter.5.cloned.1.call-done = f32[1,128,1024]{1,2,0:T(8,128)} async-done(((f32[1,512,1024]{1,2,0:T(8,128)}), f32[1,128,1024]{1,2,0:T(8,128)}) %reduce-scatter.5.cloned.1.call-update) | async-done | bytes 524304 | tf_op jit(solution)/shard_map/reduce_scatter | solution.py:54
  316.3 13.4 %convolution_bitcast_fusion.1 = f32[1,128,2048]{2,1,0:T(8,128)} fusion(f32[2048,1024]{1,0:T(8,128)} %all-gather.7.cloned.1.call-done, f32[1,128,1024]{1,2,0:T(8,128)} %reduce-scatter.5.cloned.1.call-done), kind=kOutput, calls=%fused_computation.25 | convolution fusion | flops 3221225472 | bytes 9961472 | tf_op jit(solution)/shard_map/bvn,cn->bvc/dot_general | solution.py:56
  329.7 35.3 %reduce-scatter.7.cloned.1.call-done = f32[1,128,256]{2,1,0:T(8,128)} async-done(((f32[1,128,2048]{2,1,0:T(8,128)}), f32[1,128,256]{2,1,0:T(8,128)}) %reduce-scatter.7.cloned.1.call-update) | async-done | bytes 131088 | tf_op jit(solution)/shard_map/reduce_scatter | solution.py:55
  365.0 1.7 fusion.45
  366.8 23.6 %all-gather.11.cloned.1.call-done = f32[1,128,2048]{2,1,0:T(8,128)} async-done(((f32[1,128,256]{2,1,0:T(8,128)}), f32[1,128,2048]{2,1,0:T(8,128)}) %all-gather.11.cloned.1.call-update) | async-done | bytes 1048592 | tf_op jit(solution)/shard_map/all_gather | solution.py:19
  390.4 7.6 %convolution_bitcast_fusion.2 = f32[1,128,1024]{2,1,0:T(8,128)S(1)} fusion(f32[2048,1024]{1,0:T(8,128)} %all-gather.7.cloned.1.call-done, f32[1,128,2048]{2,1,0:T(8,128)} %all-gather.11.cloned.1.call-done), kind=kOutput, calls=%fused_computation.46 | convolution fusion | flops 3221225472 | bytes 9961472 | tf_op jit(solution)/shard_map/bvc,cn->bvn/dot_general | solution.py:20
  398.0 1.5 collective-permute-start.3
  399.6 14.4 %collective-permute-done.3 = f32[1,128,1024]{2,1,0:T(8,128)S(1)} collective-permute-done((f32[1,128,1024]{2,1,0:T(8,128)S(1)}, f32[1,128,1024]{2,1,0:T(8,128)S(1)}, u32[]{:S(2)}, u32[]{:S(2)}) %collective-permute-start.3) | collective-permute-done | bytes 524320 | tf_op jit(solution)/shard_map/ppermute | solution.py:30
  414.0 15.0 %collective-permute-done.4 = f32[1,128,1024]{2,1,0:T(8,128)S(1)} collective-permute-done((f32[1,128,1024]{2,1,0:T(8,128)S(1)}, f32[1,128,1024]{2,1,0:T(8,128)S(1)}, u32[]{:S(2)}, u32[]{:S(2)}) %collective-permute-start.4) | collective-permute-done | bytes 524320 | tf_op jit(solution)/shard_map/ppermute | solution.py:30
  429.0 0.4 collective-permute-start.5
  429.4 14.2 %collective-permute-done.5 = f32[1,128,1024]{2,1,0:T(8,128)S(1)} collective-permute-done((f32[1,128,1024]{2,1,0:T(8,128)S(1)}, f32[1,128,1024]{2,1,0:T(8,128)S(1)}, u32[]{:S(2)}, u32[]{:S(2)}) %collective-permute-start.5) | collective-permute-done | bytes 524320 | tf_op jit(solution)/shard_map/ppermute | solution.py:30
  443.5 16.8 %fusion.13 = f32[1024,2048]{1,0:T(8,128)S(1)} fusion(f32[512,2048]{1,0:T(8,128)S(1)} %copy-done.2, s32[]{:T(128)S(6)} %select_n.13, f32[1,128,1024]{2,1,0:T(8,128)S(1)} %collective-permute-done.5, f32[1,128,1024]{2,1,0:T(8,128)S(1)} %collective-permute-done.4, f32[1,128,1024]{2,1,0:T(8,128)S(1)} %collective-permute-done.3, ...), kind=kOutput, calls=%fused_computation.31 | convolution fusion | flops 12888571904 | bytes 14680068 | tf_op jit(solution)/shard_map/vm,bvn->bmn/dot_general | solution.py:39
  460.4 15.3 %fusion.33 = f32[1,512,1024]{1,2,0:T(8,128)} fusion(f32[512,2048]{1,0:T(8,128)S(1)} %copy-done.2, f32[1024,2048]{1,0:T(8,128)S(1)} %fusion.13, f32[2048,1024]{0,1:T(8,128)S(1)} %bitcast.84), kind=kOutput, calls=%fused_computation.45 | convolution fusion | flops 12886999040 | bytes 23068672 | tf_op jit(solution)/shard_map/vm,bmn->bvn/dot_general | solution.py:47
  475.8 0.3 reduce-scatter.11.cloned.1.call-start
  476.0 40.7 %reduce-scatter.9.cloned.1.call-done = f32[1,128,1024]{1,2,0:T(8,128)} async-done(((f32[1,512,1024]{1,2,0:T(8,128)}), f32[1,128,1024]{1,2,0:T(8,128)}) %reduce-scatter.9.cloned.1.call-update) | async-done | bytes 524304 | tf_op jit(solution)/shard_map/reduce_scatter | solution.py:54
  516.8 13.4 %convolution_bitcast_fusion = f32[1,128,2048]{2,1,0:T(8,128)} fusion(f32[2048,1024]{1,0:T(8,128)} %all-gather.7.cloned.1.call-done, f32[1,128,1024]{1,2,0:T(8,128)} %reduce-scatter.9.cloned.1.call-done), kind=kOutput, calls=%fused_computation.24 | convolution fusion | flops 3221225472 | bytes 9961472 | tf_op jit(solution)/shard_map/bvn,cn->bvc/dot_general | solution.py:56
  530.2 35.3 %reduce-scatter.11.cloned.1.call-done = f32[1,128,256]{2,1,0:T(8,128)} async-done(((f32[1,128,2048]{2,1,0:T(8,128)}), f32[1,128,256]{2,1,0:T(8,128)}) %reduce-scatter.11.cloned.1.call-update) | async-done | bytes 131088 | tf_op jit(solution)/shard_map/reduce_scatter | solution.py:55
  565.5 1.7 fusion.44
  (34 shorter events, 0.4 us)
Async XLA Ops:
  6.5 28.9 %all-gather.5.cloned.1.call-start = ((), (), s32[]{:S(2)}) async-start(), calls=%async_computation.4 | async-start | bytes 1179648 | tf_op jit(solution)/shard_map/all_gather | solution.py:19
  7.3 179.4 %all-gather.7.cloned.1.call-start = ((), (), s32[]{:S(2)}) async-start(), calls=%async_computation.5 | async-start | bytes 10485760 | tf_op jit(solution)/shard_map/all_gather | solution.py:13
  8.0 225.9 %all-gather.9.cloned.1.call-start = ((), (), s32[]{:S(2)}) async-start(), calls=%async_computation.6 | async-start | bytes 4718592 | tf_op jit(solution)/shard_map/all_gather | solution.py:14
  8.7 307.6 %reduce-scatter.5.cloned.1.call-start = ((), (), s32[]{:S(2)}) async-start(), calls=%async_computation.7 | async-start | bytes 2621440 | tf_op jit(solution)/shard_map/reduce_scatter | solution.py:54
  194.2 15.7 %collective-permute-start = (f32[1,128,1024]{2,1,0:T(8,128)S(1)}, f32[1,128,1024]{2,1,0:T(8,128)S(1)}, u32[]{:S(2)}, u32[]{:S(2)}) collective-permute-start(f32[1,128,1024]{2,1,0:T(8,128)S(1)} %convolution_bitcast_fusion.3), channel_id=1, source_target_pairs={{0,1},{1,2},{2,3},{3,0},{4,5},{5,6},{6,7},{7,4},{8,9},{9,10},{10,1... | collective-permute-start | bytes 1572872 | tf_op jit(solution)/shard_map/ppermute | solution.py:30
  209.8 14.8 %collective-permute-start.1 = (f32[1,128,1024]{2,1,0:T(8,128)S(1)}, f32[1,128,1024]{2,1,0:T(8,128)S(1)}, u32[]{:S(2)}, u32[]{:S(2)}) collective-permute-start(f32[1,128,1024]{2,1,0:T(8,128)S(1)} %collective-permute-done), channel_id=1, source_target_pairs={{0,1},{1,2},{2,3},{3,0},{4,5},{5,6},{6,7},{7,4},{8,9},{9,10},{10,1... | collective-permute-start | bytes 1572872 | tf_op jit(solution)/shard_map/ppermute | solution.py:30
  224.6 14.1 %collective-permute-start.2 = (f32[1,128,1024]{2,1,0:T(8,128)S(1)}, f32[1,128,1024]{2,1,0:T(8,128)S(1)}, u32[]{:S(2)}, u32[]{:S(2)}) collective-permute-start(f32[1,128,1024]{2,1,0:T(8,128)S(1)} %collective-permute-done.1), channel_id=1, source_target_pairs={{0,1},{1,2},{2,3},{3,0},{4,5},{5,6},{6,7},{7,4},{8,9},{9,10},{10,1... | collective-permute-start | bytes 1572872 | tf_op jit(solution)/shard_map/ppermute | solution.py:30
  233.9 24.9 %copy-start.1 = (f32[512,2048]{1,0:T(8,128)S(1)}, f32[512,2048]{1,0:T(8,128)}, u32[]{:S(2)}) copy-start(f32[512,2048]{1,0:T(8,128)} %all-gather.9.cloned.1.call-done) | copy-start | bytes 12582916
  238.7 20.1 %copy-start = (f32[2048,1024]{0,1:T(8,128)S(1)}, f32[2048,1024]{0,1:T(8,128)}, u32[]{:S(2)}) copy-start(f32[2048,1024]{0,1:T(8,128)} %copy.7) | copy-start | bytes 25165828
  274.4 90.7 %copy-start.3 = (f32[1,128,256]{2,1,0:T(8,128)S(1)}, f32[1,128,256]{2,1,0:T(8,128)}, u32[]{:S(2)}) copy-start(f32[1,128,256]{2,1,0:T(8,128)} %param.8) | copy-start | bytes 393220
  274.4 90.6 %copy-start.5 = (f32[256]{0:T(256)S(1)}, f32[256]{0:T(256)}, u32[]{:S(2)}) copy-start(f32[256]{0:T(256)} %param.10) | copy-start | bytes 3076
  274.4 90.6 %copy-start.6 = (f32[128]{0:T(128)S(1)}, f32[128]{0:T(128)}, u32[]{:S(2)}) copy-start(f32[128]{0:T(128)} %param.9) | copy-start | bytes 1540
  274.4 90.6 %reduce-scatter.7.cloned.1.call-start = ((), (), s32[]{:S(2)}) async-start(), calls=%async_computation.8 | async-start | bytes 1179648 | tf_op jit(solution)/shard_map/reduce_scatter | solution.py:55
  329.7 60.7 %all-gather.11.cloned.1.call-start = ((), (), s32[]{:S(2)}) async-start(), calls=%async_computation.9 | async-start | bytes 1179648 | tf_op jit(solution)/shard_map/all_gather | solution.py:19
  366.7 150.0 %reduce-scatter.9.cloned.1.call-start = ((), (), s32[]{:S(2)}) async-start(), calls=%async_computation.10 | async-start | bytes 2621440 | tf_op jit(solution)/shard_map/reduce_scatter | solution.py:54
  390.4 53.2 %copy-start.2 = (f32[512,2048]{1,0:T(8,128)S(1)}, f32[512,2048]{1,0:T(8,128)}, u32[]{:S(2)}) copy-start(f32[512,2048]{1,0:T(8,128)} %all-gather.9.cloned.1.call-done) | copy-start | bytes 12582916
  390.4 70.0 %slice-start = ((s8[8388608]{0:T(1024)(128)(4,1)}), s8[4194304]{0:T(1024)(128)(4,1)S(1)}, s32[]{:S(2)}) async-start(s8[8388608]{0:T(1024)(128)(4,1)} %bitcast.83), calls=%async_computation.12 | async-start | bytes 8388608
  398.0 62.4 %slice-start.1 = ((s8[8388608]{0:T(1024)(128)(4,1)}), s8[4194304]{0:T(1024)(128)(4,1)S(1)}, s32[]{:S(2)}) async-start(s8[8388608]{0:T(1024)(128)(4,1)} %bitcast.83), calls=%async_computation.13 | async-start | bytes 8388608
  398.0 15.9 %collective-permute-start.3 = (f32[1,128,1024]{2,1,0:T(8,128)S(1)}, f32[1,128,1024]{2,1,0:T(8,128)S(1)}, u32[]{:S(2)}, u32[]{:S(2)}) collective-permute-start(f32[1,128,1024]{2,1,0:T(8,128)S(1)} %convolution_bitcast_fusion.2), channel_id=1, source_target_pairs={{0,1},{1,2},{2,3},{3,0},{4,5},{5,6},{6,7},{7,4},{8,9},{9,10},{10,1... | collective-permute-start | bytes 1572872 | tf_op jit(solution)/shard_map/ppermute | solution.py:30
  414.0 15.0 %collective-permute-start.4 = (f32[1,128,1024]{2,1,0:T(8,128)S(1)}, f32[1,128,1024]{2,1,0:T(8,128)S(1)}, u32[]{:S(2)}, u32[]{:S(2)}) collective-permute-start(f32[1,128,1024]{2,1,0:T(8,128)S(1)} %collective-permute-done.3), channel_id=1, source_target_pairs={{0,1},{1,2},{2,3},{3,0},{4,5},{5,6},{6,7},{7,4},{8,9},{9,10},{10,1... | collective-permute-start | bytes 1572872 | tf_op jit(solution)/shard_map/ppermute | solution.py:30
  429.0 14.6 %collective-permute-start.5 = (f32[1,128,1024]{2,1,0:T(8,128)S(1)}, f32[1,128,1024]{2,1,0:T(8,128)S(1)}, u32[]{:S(2)}, u32[]{:S(2)}) collective-permute-start(f32[1,128,1024]{2,1,0:T(8,128)S(1)} %collective-permute-done.4), channel_id=1, source_target_pairs={{0,1},{1,2},{2,3},{3,0},{4,5},{5,6},{6,7},{7,4},{8,9},{9,10},{10,1... | collective-permute-start | bytes 1572872 | tf_op jit(solution)/shard_map/ppermute | solution.py:30
  475.8 89.8 %copy-start.4 = (f32[1,128,256]{2,1,0:T(8,128)S(1)}, f32[1,128,256]{2,1,0:T(8,128)}, u32[]{:S(2)}) copy-start(f32[1,128,256]{2,1,0:T(8,128)} %reduce-scatter.7.cloned.1.call-done) | copy-start | bytes 393220
  475.8 89.8 %reduce-scatter.11.cloned.1.call-start = ((), (), s32[]{:S(2)}) async-start(), calls=%async_computation.11 | async-start | bytes 1179648 | tf_op jit(solution)/shard_map/reduce_scatter | solution.py:55
Sparse Core Ops, SparseCore 0:
  9.2 26.1 all-gather.4
  37.0 149.5 all-gather.6
  188.5 34.7 all-gather.8
  274.5 41.7 reduce-scatter.4
  329.8 35.1 reduce-scatter.6
  366.8 23.4 all-gather.10
  475.9 40.8 reduce-scatter.8
  530.3 35.1 reduce-scatter.10
